TPU v7x, 256 devices: a whole 4x4x8 slice. The times are simulated.
256 devices in a mesh: dp: 8 (over x, z_hi), pipe: 4 (over z_lo), expert: 8 (over y, core).
Axes of the slice: x: 4, y: 4, z: 8 (z_hi: 2, z_lo: 4; z = z_hi * 4 + z_lo), core: 2. Of those that a mesh axis runs over, the one named last changes fastest.
Arguments:
- tokens: bfloat16 [8192, 2048], P(('dp', 'expert')), may hold values from -6 to 6
- cotangent: bfloat16 [8192, 2048], P(('dp', 'expert')), may hold values from -6 to 6
- owner_ids: int32 [4, 8192, 4], P('pipe', ('dp', 'expert')), may hold values from 0 to 63, all different within a row; in each aligned block of 32 rows (0 to 31, 32 to 63, ..., all dimensions but the last counted through in order) at most 3 rows name the same one
- gate_weights: bfloat16 [4, 8192, 4], P('pipe', ('dp', 'expert')), may hold values from 0.049804688 to 0.25
- norm_gain: float32 [4, 2048], P('pipe'), may hold values from 0.5 to 1.5
- w_gate: bfloat16 [4, 64, 2048, 384], P('pipe', ('dp', 'expert')), may hold values from -0.125 to 0.125
- w_up: bfloat16 [4, 64, 2048, 384], P('pipe', ('dp', 'expert')), may hold values from -0.125 to 0.125
- w_down: bfloat16 [4, 64, 384, 2048], P('pipe', ('dp', 'expert')), may hold values from -0.3125 to 0.3125
Outputs:
- segment_out: bfloat16 [4, 8192, 2048], P('pipe', ('dp', 'expert'))
- segment_grad: bfloat16 [4, 8192, 2048], P('pipe', ('dp', 'expert'))
- gain_grad: float32 [4, 2048], P('pipe')
Inputs may be any that keep to these rules, and one draw needn't show every extreme that they name: `owner_ids`: each row names 4 different owners. In each aligned block of 32 rows (layers in order, then tokens) no owner is named by more than 3 rows, and that bound is reached.
All inputs are finite; a program needn't handle non-finite values.
Results may differ from a plain program's by a relative error of at most 0.014.
Values may be sent and summed in bfloat16 or wider, within the bound.
A program may use at most 128 MiB of HBM per device.

v0:
```python
import jax
import jax.numpy as jnp
from jax import lax
from jax.sharding import PartitionSpec as P

MICRO = 4


epsilon = 1e-06


def from_behind(value, axis, steps):
    count = lax.axis_size(axis)
    leading, last = (max(0, -steps), min(count, count - steps))
    return lax.ppermute(value, axis, [(source, source + steps) for source in range(leading, last)])


def inverse_rms(values):
    return lax.rsqrt(jnp.mean(values * values, axis=-1, keepdims=True) + epsilon)


def contract_last(left, right):
    return lax.dot_general(
        left, right, (((1,), (1,)), ((), ())), preferred_element_type=jnp.float32
    )


def route_tables(ids_part, owners, capacity):
    owner_range = jnp.arange(owners, dtype=jnp.int32)
    onehot = (ids_part[:, :, None] == owner_range[None, None, :]).astype(jnp.int32)
    member = jnp.sum(onehot, axis=1)
    position = jnp.cumsum(member, axis=0) - member
    slot_range = jnp.arange(capacity, dtype=jnp.int32)
    placed = (position[:, :, None] == slot_range[None, None, :]) & (member[:, :, None] > 0)
    placing = jnp.transpose(placed, (1, 2, 0)).astype(jnp.bfloat16)
    return (onehot.astype(jnp.float32), placing)


def gate_slots(onehot, gates_part, placing, experts_here):
    gate_pairs = gates_part.astype(jnp.float32).reshape(gates_part.shape[0], -1, experts_here)
    chosen = jnp.einsum("rjo,rjc->roc", onehot, gate_pairs)
    return jnp.einsum("okr,roc->okc", placing.astype(jnp.float32), chosen).astype(jnp.bfloat16)


def send_rows(row_block, pair_block):
    got_rows, got_pairs = (
        lax.all_to_all(row_block, ("dp", "expert"), split_axis=0, concat_axis=0, tiled=True),
        lax.all_to_all(pair_block, ("dp", "expert"), split_axis=0, concat_axis=0, tiled=True),
    )
    return (got_rows, got_pairs)


def return_rows(row_block):
    return lax.all_to_all(row_block, ("dp", "expert"), split_axis=0, concat_axis=0, tiled=True)


def send_grads(row_block):
    return lax.all_to_all(row_block, ("dp", "expert"), split_axis=0, concat_axis=0, tiled=True)


def return_grads(row_block):
    return lax.all_to_all(row_block, ("dp", "expert"), split_axis=0, concat_axis=0, tiled=True)


def expert_forward(flat_rows, flat_pairs, joint_mats, down_mats):
    hidden_width = down_mats.shape[1]
    joint_pre = jnp.dot(flat_rows, joint_mats[0], preferred_element_type=jnp.float32)
    gate_pre = joint_pre[:, :hidden_width]
    up_pre = joint_pre[:, hidden_width:]
    hidden = (jax.nn.silu(gate_pre) * up_pre).astype(jnp.bfloat16)
    projected = jnp.dot(hidden, down_mats[0], preferred_element_type=jnp.float32)
    term = flat_pairs.astype(jnp.float32) * projected
    kept_both = [joint_pre]
    return (term.astype(jnp.bfloat16), jnp.stack(kept_both))


def expert_backward(grad_rows, flat_pairs, joint_keep, joint_mats, down_mats):
    hidden_width = down_mats.shape[1]
    q_vals = contract_last(grad_rows, down_mats[0])
    gate_pre = joint_keep[0][:, :hidden_width]
    up_pre = joint_keep[0][:, hidden_width:]
    sigma = jax.nn.sigmoid(gate_pre)
    weight = flat_pairs.astype(jnp.float32)
    d_gate = (q_vals * weight * up_pre * sigma * (1.0 + gate_pre * (1.0 - sigma))).astype(
        jnp.bfloat16
    )
    d_up = (q_vals * weight * gate_pre * sigma).astype(jnp.bfloat16)
    joint_grad = jnp.concatenate([d_gate, d_up], axis=1)
    term = contract_last(joint_grad, joint_mats[0])
    return term.astype(jnp.bfloat16)


def body(tokens, cotangent, owner_ids, gate_weights, norm_gain, w_gate, w_up, w_down):
    segments = lax.axis_size("pipe")
    segment_index = lax.axis_index("pipe")
    owners = lax.axis_size("dp") * lax.axis_size("expert")
    tok_rows = tokens.shape[0]
    width = tokens.shape[1]
    micro_rows = tok_rows // MICRO
    route_count = owner_ids.shape[2]
    capacity = max(2, (5 * micro_rows * route_count + 4 * owners - 1) // (4 * owners))
    slot_count = owners * capacity
    gain_row = norm_gain[0]
    joint_mats = jnp.concatenate([w_gate[0], w_up[0]], axis=2)
    down_mats = w_down[0]
    layer_ids = owner_ids[0]
    layer_gates = gate_weights[0]
    experts_here = joint_mats.shape[0]
    joint_width = joint_mats.shape[2]

    def skip_forward(operands):
        return (
            jnp.zeros((slot_count, width), jnp.bfloat16),
            jnp.zeros((experts_here, slot_count, joint_width), jnp.float32),
        )

    def run_forward(operands):
        return expert_forward(operands[0], operands[1], joint_mats, down_mats)

    def skip_backward(operands):
        return jnp.zeros((slot_count, width), jnp.bfloat16)

    def run_backward(operands):
        return expert_backward(operands[0], operands[1], operands[2], joint_mats, down_mats)

    def timing(micro):
        is_valid = (micro >= 0) & (micro < MICRO)
        slot_pick = jnp.where(is_valid, micro, MICRO)
        start_row = jnp.clip(micro, 0, MICRO - 1) * micro_rows
        return (is_valid, slot_pick, start_row)

    layer_outs = jnp.zeros((MICRO + 1, micro_rows, width), jnp.bfloat16)
    layer_ins = jnp.zeros((MICRO + 1, micro_rows, width), jnp.bfloat16)
    kept_joint = jnp.zeros((MICRO + 1, experts_here, slot_count, joint_width), jnp.float32)
    kept_pairs = jnp.zeros((MICRO + 1, slot_count, experts_here), jnp.bfloat16)
    grad_outs = jnp.zeros((MICRO + 1, micro_rows, width), jnp.bfloat16)
    gain_sum = jnp.zeros((width,), jnp.float32)
    ticks = MICRO + segments - 1
    incoming = jnp.zeros((micro_rows, width), jnp.bfloat16)
    for tick_num in range(ticks):
        forward_is_valid, forward_slot_pick, forward_start_row = timing(tick_num - segment_index)
        forward_own_part = lax.dynamic_slice_in_dim(tokens, forward_start_row, micro_rows, 0)
        forward_layer_in = jnp.where(segment_index == 0, forward_own_part, incoming)
        forward_ids_part = lax.dynamic_slice_in_dim(layer_ids, forward_start_row, micro_rows, 0)
        gates_part = lax.dynamic_slice_in_dim(layer_gates, forward_start_row, micro_rows, 0)
        forward_x_float = forward_layer_in.astype(jnp.float32)
        forward_scale = inverse_rms(forward_x_float)
        normed = (forward_x_float * forward_scale * gain_row).astype(jnp.bfloat16)
        forward_onehot, forward_placing = route_tables(forward_ids_part, owners, capacity)
        row_block = jnp.einsum(
            "okr,rd->okd", forward_placing, normed, preferred_element_type=jnp.float32
        ).astype(jnp.bfloat16)
        pair_block = gate_slots(forward_onehot, gates_part, forward_placing, experts_here)
        f_valid, f_pick, layer_in, x_float, f_placing, row_block, pair_block = (
            forward_is_valid,
            forward_slot_pick,
            forward_layer_in,
            forward_x_float,
            forward_placing,
            row_block,
            pair_block,
        )
        got_rows, got_pairs = send_rows(row_block, pair_block)
        flat_rows = got_rows.reshape(slot_count, width)
        flat_pairs = got_pairs.reshape(slot_count, experts_here)
        result, joint_pre = lax.cond(f_valid, run_forward, skip_forward, (flat_rows, flat_pairs))
        returned = return_rows(result.reshape(owners, capacity, width))
        branch = jnp.einsum("okr,okd->rd", f_placing, returned, preferred_element_type=jnp.float32)
        layer_out = (x_float + branch).astype(jnp.bfloat16)
        layer_outs = lax.dynamic_update_index_in_dim(layer_outs, layer_out, f_pick, 0)
        layer_ins = lax.dynamic_update_index_in_dim(layer_ins, layer_in, f_pick, 0)
        kept_joint = lax.dynamic_update_index_in_dim(kept_joint, joint_pre, f_pick, 0)
        kept_pairs = lax.dynamic_update_index_in_dim(kept_pairs, flat_pairs, f_pick, 0)
        if tick_num + 1 < ticks:
            incoming = from_behind(layer_out, "pipe", 1)
    incoming = jnp.zeros((micro_rows, width), jnp.bfloat16)
    for tick_num in range(ticks):
        backward_is_valid, backward_slot_pick, backward_start_row = timing(
            tick_num - (segments - 1 - segment_index)
        )
        own_part = lax.dynamic_slice_in_dim(cotangent, backward_start_row, micro_rows, 0)
        backward_grad_in = jnp.where(segment_index == segments - 1, own_part, incoming)
        ids_part = lax.dynamic_slice_in_dim(layer_ids, backward_start_row, micro_rows, 0)
        backward_layer_in = lax.dynamic_index_in_dim(
            layer_ins, backward_slot_pick, 0, keepdims=False
        )
        backward_x_float = backward_layer_in.astype(jnp.float32)
        backward_scale = inverse_rms(backward_x_float)
        onehot, backward_placing = route_tables(ids_part, owners, capacity)
        grad_block = jnp.einsum(
            "okr,rd->okd", backward_placing, backward_grad_in, preferred_element_type=jnp.float32
        ).astype(jnp.bfloat16)
        b_valid, b_pick, grad_in, bx_float, b_scale, b_placing, grad_block = (
            backward_is_valid,
            backward_slot_pick,
            backward_grad_in,
            backward_x_float,
            backward_scale,
            backward_placing,
            grad_block,
        )
        got_grads = send_grads(grad_block).reshape(slot_count, width)
        joint_keep = lax.dynamic_index_in_dim(kept_joint, b_pick, 0, keepdims=False)
        pair_keep = lax.dynamic_index_in_dim(kept_pairs, b_pick, 0, keepdims=False)
        owner_grad = lax.cond(
            b_valid, run_backward, skip_backward, (got_grads, pair_keep, joint_keep)
        )
        returned = return_grads(owner_grad.reshape(owners, capacity, width))
        normed_grad = jnp.einsum(
            "okr,okd->rd", b_placing, returned, preferred_element_type=jnp.float32
        )
        weighted = gain_row * normed_grad
        grad_x = (
            grad_in.astype(jnp.float32)
            + b_scale * weighted
            - bx_float
            * b_scale
            * b_scale
            * b_scale
            * jnp.mean(weighted * bx_float, axis=-1, keepdims=True)
        )
        gain_term = jnp.where(b_valid, jnp.sum(normed_grad * bx_float * b_scale, axis=0), 0.0)
        grad_bf, gain_term = (grad_x.astype(jnp.bfloat16), gain_term)
        grad_outs = lax.dynamic_update_index_in_dim(grad_outs, grad_bf, b_pick, 0)
        gain_sum = gain_sum + gain_term
        if tick_num + 1 < ticks:
            incoming = from_behind(grad_bf, "pipe", -1)
    gain_grad = lax.psum(gain_sum, ("dp", "expert"))
    segment_out = layer_outs[:MICRO].reshape(1, tok_rows, width)
    segment_grad = grad_outs[:MICRO].reshape(1, tok_rows, width)
    return (segment_out, segment_grad, gain_grad.reshape(1, width))


def solution(mesh):
    in_specs = (
        P(("dp", "expert"), None),
        P(("dp", "expert"), None),
        P("pipe", ("dp", "expert"), None),
        P("pipe", ("dp", "expert"), None),
        P("pipe", None),
        P("pipe", ("dp", "expert"), None, None),
        P("pipe", ("dp", "expert"), None, None),
        P("pipe", ("dp", "expert"), None, None),
    )
    out_specs = (
        P("pipe", ("dp", "expert"), None),
        P("pipe", ("dp", "expert"), None),
        P("pipe", None),
    )
    return jax.shard_map(body, mesh=mesh, in_specs=in_specs, out_specs=out_specs, check_vma=False)
```

profile of v0, /device:TPU:1, one launch (start us, length us, event | category | flops | bytes accessed | tf_op | source)
XLA Modules:
  0.0 1507.8 jit_solution(17595029229092546663)
XLA Ops:
  5.5 15.6 %all-to-all-start = ((bf16[64,3,1]{1,2,0:T(2,128)(2,1)}), bf16[64,3,1]{1,2,0:T(2,128)(2,1)S(1)}, u32[]{:S(2)}, u32[]{:S(2)}) async-start(bf16[64,3,1]{1,2,0:T(2,128)(2,1)} %copy.214), calls=%async_computation | async-start | bytes 65536 | tf_op jit(solution)/shard_map/all_to_all | solution.py:48
  25.2 7.5 all-to-all-done
  40.4 25.5 %all-to-all-done.1 = bf16[64,3,2048]{2,1,0:T(4,128)(2,1)} async-done(((bf16[64,3,2048]{2,1,0:T(4,128)(2,1)}), bf16[64,3,2048]{2,1,0:T(4,128)(2,1)}, u32[]{:S(2)}, u32[]{:S(2)}) %all-to-all-start.1) | async-done | bytes 786464 | tf_op jit(solution)/shard_map/all_to_all | solution.py:47
  65.9 9.1 conditional.14
  84.8 18.1 %all-to-all-done.2 = bf16[64,3,2048]{2,1,0:T(4,128)(2,1)} async-done(((bf16[64,3,2048]{2,1,0:T(4,128)(2,1)}), bf16[64,3,2048]{2,1,0:T(4,128)(2,1)}, u32[]{:S(2)}, u32[]{:S(2)}) %all-to-all-start.2) | async-done | bytes 786464 | tf_op jit(solution)/shard_map/all_to_all | solution.py:54
  109.9 7.3 collective-permute-start
  122.4 14.5 all-to-all-start.4
  136.9 28.5 %all-to-all-done.4 = bf16[64,3,2048]{2,1,0:T(4,128)(2,1)} async-done(((bf16[64,3,2048]{2,1,0:T(4,128)(2,1)}), bf16[64,3,2048]{2,1,0:T(4,128)(2,1)}, u32[]{:S(2)}, u32[]{:S(2)}) %all-to-all-start.4) | async-done | bytes 786464 | tf_op jit(solution)/shard_map/all_to_all | solution.py:47
  165.4 9.3 conditional.15
  184.1 18.4 %all-to-all-done.5 = bf16[64,3,2048]{2,1,0:T(4,128)(2,1)} async-done(((bf16[64,3,2048]{2,1,0:T(4,128)(2,1)}), bf16[64,3,2048]{2,1,0:T(4,128)(2,1)}, u32[]{:S(2)}, u32[]{:S(2)}) %all-to-all-start.5) | async-done | bytes 786464 | tf_op jit(solution)/shard_map/all_to_all | solution.py:54
  205.4 17.4 %collective-permute-start.1 = (bf16[32,2048]{1,0:T(8,128)(2,1)S(1)}, bf16[32,2048]{1,0:T(8,128)(2,1)S(1)}, u32[]{:S(2)}, u32[]{:S(2)}) collective-permute-start(bf16[32,2048]{1,0:T(8,128)(2,1)S(1)} %get-tuple-element.841), channel_id=1, source_target_pairs={{0,8},{8,16},{16,24},{1,9},{9,17},{17,25},{2,10},{10,18},{18,26},{... | collective-permute-start | bytes 393224 | tf_op jit(solution)/shard_map/ppermute | solution.py:15
  233.7 7.2 all-to-all-done.6
  240.8 5.9 all-to-all-start.7
  246.7 28.6 %all-to-all-done.7 = bf16[64,3,2048]{2,1,0:T(4,128)(2,1)} async-done(((bf16[64,3,2048]{2,1,0:T(4,128)(2,1)}), bf16[64,3,2048]{2,1,0:T(4,128)(2,1)}, u32[]{:S(2)}, u32[]{:S(2)}) %all-to-all-start.7) | async-done | bytes 786464 | tf_op jit(solution)/shard_map/all_to_all | solution.py:47
  275.3 9.1 conditional.16
  287.7 9.0 all-to-all-start.8
  298.6 20.2 %all-to-all-done.8 = bf16[64,3,2048]{2,1,0:T(4,128)(2,1)} async-done(((bf16[64,3,2048]{2,1,0:T(4,128)(2,1)}), bf16[64,3,2048]{2,1,0:T(4,128)(2,1)}, u32[]{:S(2)}, u32[]{:S(2)}) %all-to-all-start.8) | async-done | bytes 786464 | tf_op jit(solution)/shard_map/all_to_all | solution.py:54
  324.2 9.3 all-to-all-start.9
  338.0 7.1 all-to-all-done.9
  350.9 26.9 %all-to-all-done.10 = bf16[64,3,2048]{2,1,0:T(4,128)(2,1)} async-done(((bf16[64,3,2048]{2,1,0:T(4,128)(2,1)}), bf16[64,3,2048]{2,1,0:T(4,128)(2,1)}, u32[]{:S(2)}, u32[]{:S(2)}) %all-to-all-start.10) | async-done | bytes 786464 | tf_op jit(solution)/shard_map/all_to_all | solution.py:47
  377.8 9.1 conditional.17
  390.2 9.2 all-to-all-start.11
  399.7 21.5 %all-to-all-done.11 = bf16[64,3,2048]{2,1,0:T(4,128)(2,1)} async-done(((bf16[64,3,2048]{2,1,0:T(4,128)(2,1)}), bf16[64,3,2048]{2,1,0:T(4,128)(2,1)}, u32[]{:S(2)}, u32[]{:S(2)}) %all-to-all-start.11) | async-done | bytes 786464 | tf_op jit(solution)/shard_map/all_to_all | solution.py:54
  426.2 9.1 all-to-all-start.12
  439.9 7.1 all-to-all-done.12
  452.8 21.8 %all-to-all-done.13 = bf16[64,3,2048]{2,1,0:T(4,128)(2,1)} async-done(((bf16[64,3,2048]{2,1,0:T(4,128)(2,1)}), bf16[64,3,2048]{2,1,0:T(4,128)(2,1)}, u32[]{:S(2)}, u32[]{:S(2)}) %all-to-all-start.13) | async-done | bytes 786464 | tf_op jit(solution)/shard_map/all_to_all | solution.py:47
  486.5 24.1 %all-to-all-done.14 = bf16[64,3,2048]{2,1,0:T(4,128)(2,1)} async-done(((bf16[64,3,2048]{2,1,0:T(4,128)(2,1)}), bf16[64,3,2048]{2,1,0:T(4,128)(2,1)}, u32[]{:S(2)}, u32[]{:S(2)}) %all-to-all-start.14) | async-done | bytes 786464 | tf_op jit(solution)/shard_map/all_to_all | solution.py:54
  517.5 7.1 all-to-all-start.15
  529.1 7.2 all-to-all-done.15
  542.1 22.4 %all-to-all-done.16 = bf16[64,3,2048]{2,1,0:T(4,128)(2,1)} async-done(((bf16[64,3,2048]{2,1,0:T(4,128)(2,1)}), bf16[64,3,2048]{2,1,0:T(4,128)(2,1)}, u32[]{:S(2)}, u32[]{:S(2)}) %all-to-all-start.16) | async-done | bytes 786464 | tf_op jit(solution)/shard_map/all_to_all | solution.py:47
  569.6 9.2 all-to-all-start.17
  580.6 26.7 %all-to-all-done.17 = bf16[64,3,2048]{2,1,0:T(4,128)(2,1)} async-done(((bf16[64,3,2048]{2,1,0:T(4,128)(2,1)}), bf16[64,3,2048]{2,1,0:T(4,128)(2,1)}, u32[]{:S(2)}, u32[]{:S(2)}) %all-to-all-start.17) | async-done | bytes 786464 | tf_op jit(solution)/shard_map/all_to_all | solution.py:54
  612.5 7.5 all-to-all-start.18
  624.5 7.1 all-to-all-done.18
  642.5 23.4 %all-to-all-done.19 = bf16[64,3,2048]{2,1,0:T(4,128)(2,1)} async-done(((bf16[64,3,2048]{2,1,0:T(4,128)(2,1)}), bf16[64,3,2048]{2,1,0:T(4,128)(2,1)}, u32[]{:S(2)}, u32[]{:S(2)}) %all-to-all-start.19) | async-done | bytes 786464 | tf_op jit(solution)/shard_map/all_to_all | solution.py:47
  701.7 20.6 %all-to-all-done.22 = bf16[64,3,2048]{2,1,0:T(4,128)(2,1)} async-done(((bf16[64,3,2048]{2,1,0:T(4,128)(2,1)}), bf16[64,3,2048]{2,1,0:T(4,128)(2,1)}, u32[]{:S(2)}, u32[]{:S(2)}) %all-to-all-start.22) | async-done | bytes 786464 | tf_op jit(solution)/shard_map/all_to_all | solution.py:62
  728.1 14.4 collective-permute-done.6
  750.4 28.5 %all-to-all-done.23 = bf16[64,3,2048]{2,1,0:T(4,128)(2,1)} async-done(((bf16[64,3,2048]{2,1,0:T(4,128)(2,1)}), bf16[64,3,2048]{2,1,0:T(4,128)(2,1)}, u32[]{:S(2)}, u32[]{:S(2)}) %all-to-all-start.23) | async-done | bytes 786464 | tf_op jit(solution)/shard_map/all_to_all | solution.py:58
  788.4 19.0 %all-to-all-done.24 = bf16[64,3,2048]{2,1,0:T(4,128)(2,1)} async-done(((bf16[64,3,2048]{2,1,0:T(4,128)(2,1)}), bf16[64,3,2048]{2,1,0:T(4,128)(2,1)}, u32[]{:S(2)}, u32[]{:S(2)}) %all-to-all-start.24) | async-done | bytes 786464 | tf_op jit(solution)/shard_map/all_to_all | solution.py:62
  812.8 11.5 collective-permute-done.7
  827.4 12.2 all-to-all-start.25
  839.6 28.5 %all-to-all-done.25 = bf16[64,3,2048]{2,1,0:T(4,128)(2,1)} async-done(((bf16[64,3,2048]{2,1,0:T(4,128)(2,1)}), bf16[64,3,2048]{2,1,0:T(4,128)(2,1)}, u32[]{:S(2)}, u32[]{:S(2)}) %all-to-all-start.25) | async-done | bytes 786464 | tf_op jit(solution)/shard_map/all_to_all | solution.py:58
  877.8 19.0 %all-to-all-done.26 = bf16[64,3,2048]{2,1,0:T(4,128)(2,1)} async-done(((bf16[64,3,2048]{2,1,0:T(4,128)(2,1)}), bf16[64,3,2048]{2,1,0:T(4,128)(2,1)}, u32[]{:S(2)}, u32[]{:S(2)}) %all-to-all-start.26) | async-done | bytes 786464 | tf_op jit(solution)/shard_map/all_to_all | solution.py:62
  902.2 17.1 %collective-permute-done.8 = bf16[32,2048]{1,0:T(8,128)(2,1)S(1)} collective-permute-done((bf16[32,2048]{1,0:T(8,128)(2,1)S(1)}, bf16[32,2048]{1,0:T(8,128)(2,1)S(1)}, u32[]{:S(2)}, u32[]{:S(2)}) %collective-permute-start.8) | collective-permute-done | bytes 131104 | tf_op jit(solution)/shard_map/ppermute | solution.py:15
  922.4 7.8 all-to-all-start.27
  930.2 28.5 %all-to-all-done.27 = bf16[64,3,2048]{2,1,0:T(4,128)(2,1)} async-done(((bf16[64,3,2048]{2,1,0:T(4,128)(2,1)}), bf16[64,3,2048]{2,1,0:T(4,128)(2,1)}, u32[]{:S(2)}, u32[]{:S(2)}) %all-to-all-start.27) | async-done | bytes 786464 | tf_op jit(solution)/shard_map/all_to_all | solution.py:58
  958.6 9.7 conditional.24
  976.9 19.1 %all-to-all-done.28 = bf16[64,3,2048]{2,1,0:T(4,128)(2,1)} async-done(((bf16[64,3,2048]{2,1,0:T(4,128)(2,1)}), bf16[64,3,2048]{2,1,0:T(4,128)(2,1)}, u32[]{:S(2)}, u32[]{:S(2)}) %all-to-all-start.28) | async-done | bytes 786464 | tf_op jit(solution)/shard_map/all_to_all | solution.py:62
  1001.6 7.8 collective-permute-done.9
  1012.4 7.8 all-to-all-start.29
  1020.2 28.5 %all-to-all-done.29 = bf16[64,3,2048]{2,1,0:T(4,128)(2,1)} async-done(((bf16[64,3,2048]{2,1,0:T(4,128)(2,1)}), bf16[64,3,2048]{2,1,0:T(4,128)(2,1)}, u32[]{:S(2)}, u32[]{:S(2)}) %all-to-all-start.29) | async-done | bytes 786464 | tf_op jit(solution)/shard_map/all_to_all | solution.py:58
  1048.7 9.7 conditional.25
  1066.9 19.1 %all-to-all-done.30 = bf16[64,3,2048]{2,1,0:T(4,128)(2,1)} async-done(((bf16[64,3,2048]{2,1,0:T(4,128)(2,1)}), bf16[64,3,2048]{2,1,0:T(4,128)(2,1)}, u32[]{:S(2)}, u32[]{:S(2)}) %all-to-all-start.30) | async-done | bytes 786464 | tf_op jit(solution)/shard_map/all_to_all | solution.py:62
  1091.4 23.4 %collective-permute-done.10 = bf16[32,2048]{1,0:T(8,128)(2,1)S(1)} collective-permute-done((bf16[32,2048]{1,0:T(8,128)(2,1)S(1)}, bf16[32,2048]{1,0:T(8,128)(2,1)S(1)}, u32[]{:S(2)}, u32[]{:S(2)}) %collective-permute-start.10) | collective-permute-done | bytes 131104 | tf_op jit(solution)/shard_map/ppermute | solution.py:15
  1123.6 28.0 %all-to-all-done.31 = bf16[64,3,2048]{2,1,0:T(4,128)(2,1)} async-done(((bf16[64,3,2048]{2,1,0:T(4,128)(2,1)}), bf16[64,3,2048]{2,1,0:T(4,128)(2,1)}, u32[]{:S(2)}, u32[]{:S(2)}) %all-to-all-start.31) | async-done | bytes 786464 | tf_op jit(solution)/shard_map/all_to_all | solution.py:58
  1151.6 9.7 conditional.26
  1170.2 27.8 %all-to-all-done.32 = bf16[64,3,2048]{2,1,0:T(4,128)(2,1)} async-done(((bf16[64,3,2048]{2,1,0:T(4,128)(2,1)}), bf16[64,3,2048]{2,1,0:T(4,128)(2,1)}, u32[]{:S(2)}, u32[]{:S(2)}) %all-to-all-start.32) | async-done | bytes 786464 | tf_op jit(solution)/shard_map/all_to_all | solution.py:62
  1211.5 10.1 all-to-all-start.33
  1224.8 18.5 %all-to-all-done.33 = bf16[64,3,2048]{2,1,0:T(4,128)(2,1)} async-done(((bf16[64,3,2048]{2,1,0:T(4,128)(2,1)}), bf16[64,3,2048]{2,1,0:T(4,128)(2,1)}, u32[]{:S(2)}, u32[]{:S(2)}) %all-to-all-start.33) | async-done | bytes 786464 | tf_op jit(solution)/shard_map/all_to_all | solution.py:58
  1243.3 8.0 all-to-all-start.20
  1251.3 9.8 conditional.27
  1264.4 8.6 all-to-all-done.20
  1281.5 18.8 %all-to-all-done.34 = bf16[64,3,2048]{2,1,0:T(4,128)(2,1)S(1)} async-done(((bf16[64,3,2048]{2,1,0:T(4,128)(2,1)}), bf16[64,3,2048]{2,1,0:T(4,128)(2,1)S(1)}, u32[]{:S(2)}, u32[]{:S(2)}) %all-to-all-start.34) | async-done | bytes 786464 | tf_op jit(solution)/shard_map/all_to_all | solution.py:62
  1302.3 203.1 %psum.7 = f32[1,2048]{1,0:T(1,128)} all-reduce(f32[1,2048]{1,0:T(1,128)S(1)} %bitcast.633), channel_id=1, replica_groups=mesh['dp'=8,'pipe'=4,'expert'=8] {'dp','expert'}, use_global_device_ids=true, to_apply=%region_84.85 | all-reduce | flops 2048 | bytes 16384 | tf_op jit(solution)/shard_map/psum | solution.py:228
  (376 shorter events, 407.3 us)
Async XLA Ops:
  5.5 27.2 %all-to-all-start = ((bf16[64,3,1]{1,2,0:T(2,128)(2,1)}), bf16[64,3,1]{1,2,0:T(2,128)(2,1)S(1)}, u32[]{:S(2)}, u32[]{:S(2)}) async-start(bf16[64,3,1]{1,2,0:T(2,128)(2,1)} %copy.214), calls=%async_computation | async-start | bytes 65536 | tf_op jit(solution)/shard_map/all_to_all | solution.py:48
  32.7 33.2 %all-to-all-start.1 = ((bf16[64,3,2048]{2,1,0:T(4,128)(2,1)}), bf16[64,3,2048]{2,1,0:T(4,128)(2,1)}, u32[]{:S(2)}, u32[]{:S(2)}) async-start(bf16[64,3,2048]{2,1,0:T(4,128)(2,1)} %copy.215), calls=%async_computation.1 | async-start | bytes 2097152 | tf_op jit(solution)/shard_map/all_to_all | solution.py:47
  78.3 24.5 %all-to-all-start.2 = ((bf16[64,3,2048]{2,1,0:T(4,128)(2,1)}), bf16[64,3,2048]{2,1,0:T(4,128)(2,1)}, u32[]{:S(2)}, u32[]{:S(2)}) async-start(bf16[64,3,2048]{2,1,0:T(4,128)(2,1)} %reshape.639), calls=%async_computation.2 | async-start | bytes 2097152 | tf_op jit(solution)/shard_map/all_to_all | solution.py:54
  102.8 19.6 %all-to-all-start.3 = ((bf16[64,3,1]{1,2,0:T(2,128)(2,1)}), bf16[64,3,1]{1,2,0:T(2,128)(2,1)S(1)}, u32[]{:S(2)}, u32[]{:S(2)}) async-start(bf16[64,3,1]{1,2,0:T(2,128)(2,1)} %copy.218), calls=%async_computation.3 | async-start | bytes 65536 | tf_op jit(solution)/shard_map/all_to_all | solution.py:48
  107.5 10.6 copy-start.2
  107.6 12.7 copy-start.7
  109.9 10.4 copy-start.5
  109.9 9.6 collective-permute-start
  122.4 43.0 %all-to-all-start.4 = ((bf16[64,3,2048]{2,1,0:T(4,128)(2,1)}), bf16[64,3,2048]{2,1,0:T(4,128)(2,1)}, u32[]{:S(2)}, u32[]{:S(2)}) async-start(bf16[64,3,2048]{2,1,0:T(4,128)(2,1)} %copy.219), calls=%async_computation.4 | async-start | bytes 2097152 | tf_op jit(solution)/shard_map/all_to_all | solution.py:47
  178.0 24.5 %all-to-all-start.5 = ((bf16[64,3,2048]{2,1,0:T(4,128)(2,1)}), bf16[64,3,2048]{2,1,0:T(4,128)(2,1)}, u32[]{:S(2)}, u32[]{:S(2)}) async-start(bf16[64,3,2048]{2,1,0:T(4,128)(2,1)} %reshape.641), calls=%async_computation.5 | async-start | bytes 2097152 | tf_op jit(solution)/shard_map/all_to_all | solution.py:54
  205.4 23.7 %collective-permute-start.1 = (bf16[32,2048]{1,0:T(8,128)(2,1)S(1)}, bf16[32,2048]{1,0:T(8,128)(2,1)S(1)}, u32[]{:S(2)}, u32[]{:S(2)}) collective-permute-start(bf16[32,2048]{1,0:T(8,128)(2,1)S(1)} %get-tuple-element.841), channel_id=1, source_target_pairs={{0,8},{8,16},{16,24},{1,9},{9,17},{17,25},{2,10},{10,18},{18,26},{... | collective-permute-start | bytes 393224 | tf_op jit(solution)/shard_map/ppermute | solution.py:15
  224.3 16.5 %all-to-all-start.6 = ((bf16[64,3,1]{1,2,0:T(2,128)(2,1)}), bf16[64,3,1]{1,2,0:T(2,128)(2,1)S(1)}, u32[]{:S(2)}, u32[]{:S(2)}) async-start(bf16[64,3,1]{1,2,0:T(2,128)(2,1)} %copy.222), calls=%async_computation.6 | async-start | bytes 65536 | tf_op jit(solution)/shard_map/all_to_all | solution.py:48
  240.8 34.5 %all-to-all-start.7 = ((bf16[64,3,2048]{2,1,0:T(4,128)(2,1)}), bf16[64,3,2048]{2,1,0:T(4,128)(2,1)}, u32[]{:S(2)}, u32[]{:S(2)}) async-start(bf16[64,3,2048]{2,1,0:T(4,128)(2,1)} %copy.223), calls=%async_computation.7 | async-start | bytes 2097152 | tf_op jit(solution)/shard_map/all_to_all | solution.py:47
  284.4 12.5 copy-start.24
  287.7 31.1 %all-to-all-start.8 = ((bf16[64,3,2048]{2,1,0:T(4,128)(2,1)}), bf16[64,3,2048]{2,1,0:T(4,128)(2,1)}, u32[]{:S(2)}, u32[]{:S(2)}) async-start(bf16[64,3,2048]{2,1,0:T(4,128)(2,1)} %reshape.643), calls=%async_computation.8 | async-start | bytes 2097152 | tf_op jit(solution)/shard_map/all_to_all | solution.py:54
  321.7 11.8 collective-permute-start.2
  324.2 20.9 %all-to-all-start.9 = ((bf16[64,3,1]{1,2,0:T(2,128)(2,1)}), bf16[64,3,1]{1,2,0:T(2,128)(2,1)S(1)}, u32[]{:S(2)}, u32[]{:S(2)}) async-start(bf16[64,3,1]{1,2,0:T(2,128)(2,1)} %copy.226), calls=%async_computation.9 | async-start | bytes 65536 | tf_op jit(solution)/shard_map/all_to_all | solution.py:48
  345.1 32.7 %all-to-all-start.10 = ((bf16[64,3,2048]{2,1,0:T(4,128)(2,1)}), bf16[64,3,2048]{2,1,0:T(4,128)(2,1)}, u32[]{:S(2)}, u32[]{:S(2)}) async-start(bf16[64,3,2048]{2,1,0:T(4,128)(2,1)} %copy.227), calls=%async_computation.10 | async-start | bytes 2097152 | tf_op jit(solution)/shard_map/all_to_all | solution.py:47
  386.9 12.6 copy-start.23
  390.2 31.1 %all-to-all-start.11 = ((bf16[64,3,2048]{2,1,0:T(4,128)(2,1)}), bf16[64,3,2048]{2,1,0:T(4,128)(2,1)}, u32[]{:S(2)}, u32[]{:S(2)}) async-start(bf16[64,3,2048]{2,1,0:T(4,128)(2,1)} %reshape.645), calls=%async_computation.11 | async-start | bytes 2097152 | tf_op jit(solution)/shard_map/all_to_all | solution.py:54
  424.2 11.2 collective-permute-start.3
  426.2 20.7 %all-to-all-start.12 = ((bf16[64,3,1]{1,2,0:T(2,128)(2,1)}), bf16[64,3,1]{1,2,0:T(2,128)(2,1)S(1)}, u32[]{:S(2)}, u32[]{:S(2)}) async-start(bf16[64,3,1]{1,2,0:T(2,128)(2,1)} %copy.230), calls=%async_computation.12 | async-start | bytes 65536 | tf_op jit(solution)/shard_map/all_to_all | solution.py:48
  447.0 27.6 %all-to-all-start.13 = ((bf16[64,3,2048]{2,1,0:T(4,128)(2,1)}), bf16[64,3,2048]{2,1,0:T(4,128)(2,1)}, u32[]{:S(2)}, u32[]{:S(2)}) async-start(bf16[64,3,2048]{2,1,0:T(4,128)(2,1)} %copy.231), calls=%async_computation.13 | async-start | bytes 2097152 | tf_op jit(solution)/shard_map/all_to_all | solution.py:47
  476.6 8.9 copy-start.22
  479.9 30.7 %all-to-all-start.14 = ((bf16[64,3,2048]{2,1,0:T(4,128)(2,1)}), bf16[64,3,2048]{2,1,0:T(4,128)(2,1)}, u32[]{:S(2)}, u32[]{:S(2)}) async-start(bf16[64,3,2048]{2,1,0:T(4,128)(2,1)} %reshape.647), calls=%async_computation.14 | async-start | bytes 2097152 | tf_op jit(solution)/shard_map/all_to_all | solution.py:54
  513.5 11.1 collective-permute-start.4
  517.5 18.8 %all-to-all-start.15 = ((bf16[64,3,1]{1,2,0:T(2,128)(2,1)}), bf16[64,3,1]{1,2,0:T(2,128)(2,1)S(1)}, u32[]{:S(2)}, u32[]{:S(2)}) async-start(bf16[64,3,1]{1,2,0:T(2,128)(2,1)} %copy.234), calls=%async_computation.15 | async-start | bytes 65536 | tf_op jit(solution)/shard_map/all_to_all | solution.py:48
  536.3 28.2 %all-to-all-start.16 = ((bf16[64,3,2048]{2,1,0:T(4,128)(2,1)}), bf16[64,3,2048]{2,1,0:T(4,128)(2,1)}, u32[]{:S(2)}, u32[]{:S(2)}) async-start(bf16[64,3,2048]{2,1,0:T(4,128)(2,1)} %copy.235), calls=%async_computation.16 | async-start | bytes 2097152 | tf_op jit(solution)/shard_map/all_to_all | solution.py:47
  566.4 12.6 copy-start.21
  569.6 37.7 %all-to-all-start.17 = ((bf16[64,3,2048]{2,1,0:T(4,128)(2,1)}), bf16[64,3,2048]{2,1,0:T(4,128)(2,1)}, u32[]{:S(2)}, u32[]{:S(2)}) async-start(bf16[64,3,2048]{2,1,0:T(4,128)(2,1)} %reshape.649), calls=%async_computation.17 | async-start | bytes 2097152 | tf_op jit(solution)/shard_map/all_to_all | solution.py:54
  610.2 9.8 collective-permute-start.5
  612.5 19.1 %all-to-all-start.18 = ((bf16[64,3,1]{1,2,0:T(2,128)(2,1)}), bf16[64,3,1]{1,2,0:T(2,128)(2,1)S(1)}, u32[]{:S(2)}, u32[]{:S(2)}) async-start(bf16[64,3,1]{1,2,0:T(2,128)(2,1)} %copy.238), calls=%async_computation.18 | async-start | bytes 65536 | tf_op jit(solution)/shard_map/all_to_all | solution.py:48
  631.6 34.4 %all-to-all-start.19 = ((bf16[64,3,2048]{2,1,0:T(4,128)(2,1)}), bf16[64,3,2048]{2,1,0:T(4,128)(2,1)}, u32[]{:S(2)}, u32[]{:S(2)}) async-start(bf16[64,3,2048]{2,1,0:T(4,128)(2,1)} %copy.239), calls=%async_computation.19 | async-start | bytes 2097152 | tf_op jit(solution)/shard_map/all_to_all | solution.py:47
  666.0 24.4 %all-to-all-start.21 = ((bf16[64,3,2048]{2,1,0:T(4,128)(2,1)}), bf16[64,3,2048]{2,1,0:T(4,128)(2,1)}, u32[]{:S(2)}, u32[]{:S(2)}) async-start(bf16[64,3,2048]{2,1,0:T(4,128)(2,1)} %copy.242), calls=%async_computation.21 | async-start | bytes 2097152 | tf_op jit(solution)/shard_map/all_to_all | solution.py:58
  691.4 9.1 copy-start.20
  694.6 27.6 %copy-start.14 = (s32[64,32]{0,1:T(8,128)S(1)}, s32[64,32]{0,1:T(8,128)}, u32[]{:S(2)}) copy-start(s32[64,32]{0,1:T(8,128)} %copy-done.13) | copy-start | bytes 24580
  694.6 27.6 %all-to-all-start.22 = ((bf16[64,3,2048]{2,1,0:T(4,128)(2,1)}), bf16[64,3,2048]{2,1,0:T(4,128)(2,1)}, u32[]{:S(2)}, u32[]{:S(2)}) async-start(bf16[64,3,2048]{2,1,0:T(4,128)(2,1)} %reshape.654), calls=%async_computation.22 | async-start | bytes 2097152 | tf_op jit(solution)/shard_map/all_to_all | solution.py:62
  726.8 15.7 %collective-permute-start.6 = (bf16[32,2048]{1,0:T(8,128)(2,1)S(1)}, bf16[32,2048]{1,0:T(8,128)(2,1)S(1)}, u32[]{:S(2)}, u32[]{:S(2)}) collective-permute-start(bf16[32,2048]{1,0:T(8,128)(2,1)S(1)} %get-tuple-element.790), channel_id=1, source_target_pairs={{8,0},{16,8},{24,16},{9,1},{17,9},{25,17},{10,2},{18,10},{26,18},{... | collective-permute-start | bytes 393224 | tf_op jit(solution)/shard_map/ppermute | solution.py:15
  744.6 34.2 %all-to-all-start.23 = ((bf16[64,3,2048]{2,1,0:T(4,128)(2,1)}), bf16[64,3,2048]{2,1,0:T(4,128)(2,1)}, u32[]{:S(2)}, u32[]{:S(2)}) async-start(bf16[64,3,2048]{2,1,0:T(4,128)(2,1)} %copy.251), calls=%async_computation.23 | async-start | bytes 2097152 | tf_op jit(solution)/shard_map/all_to_all | solution.py:58
  783.1 24.3 %all-to-all-start.24 = ((bf16[64,3,2048]{2,1,0:T(4,128)(2,1)}), bf16[64,3,2048]{2,1,0:T(4,128)(2,1)}, u32[]{:S(2)}, u32[]{:S(2)}) async-start(bf16[64,3,2048]{2,1,0:T(4,128)(2,1)} %reshape.656), calls=%async_computation.24 | async-start | bytes 2097152 | tf_op jit(solution)/shard_map/all_to_all | solution.py:62
  811.5 12.8 collective-permute-start.7
  827.4 40.7 %all-to-all-start.25 = ((bf16[64,3,2048]{2,1,0:T(4,128)(2,1)}), bf16[64,3,2048]{2,1,0:T(4,128)(2,1)}, u32[]{:S(2)}, u32[]{:S(2)}) async-start(bf16[64,3,2048]{2,1,0:T(4,128)(2,1)} %copy.253), calls=%async_computation.25 | async-start | bytes 2097152 | tf_op jit(solution)/shard_map/all_to_all | solution.py:58
  869.2 8.4 copy-start.18
  872.5 24.3 %all-to-all-start.26 = ((bf16[64,3,2048]{2,1,0:T(4,128)(2,1)}), bf16[64,3,2048]{2,1,0:T(4,128)(2,1)}, u32[]{:S(2)}, u32[]{:S(2)}) async-start(bf16[64,3,2048]{2,1,0:T(4,128)(2,1)} %reshape.658), calls=%async_computation.26 | async-start | bytes 2097152 | tf_op jit(solution)/shard_map/all_to_all | solution.py:62
  900.9 18.4 %collective-permute-start.8 = (bf16[32,2048]{1,0:T(8,128)(2,1)S(1)}, bf16[32,2048]{1,0:T(8,128)(2,1)S(1)}, u32[]{:S(2)}, u32[]{:S(2)}) collective-permute-start(bf16[32,2048]{1,0:T(8,128)(2,1)S(1)} %get-tuple-element.786), channel_id=1, source_target_pairs={{8,0},{16,8},{24,16},{9,1},{17,9},{25,17},{10,2},{18,10},{26,18},{... | collective-permute-start | bytes 393224 | tf_op jit(solution)/shard_map/ppermute | solution.py:15
  922.4 36.3 %all-to-all-start.27 = ((bf16[64,3,2048]{2,1,0:T(4,128)(2,1)}), bf16[64,3,2048]{2,1,0:T(4,128)(2,1)}, u32[]{:S(2)}, u32[]{:S(2)}) async-start(bf16[64,3,2048]{2,1,0:T(4,128)(2,1)} %copy.255), calls=%async_computation.27 | async-start | bytes 2097152 | tf_op jit(solution)/shard_map/all_to_all | solution.py:58
  968.3 8.4 copy-start.17
  971.6 24.4 %all-to-all-start.28 = ((bf16[64,3,2048]{2,1,0:T(4,128)(2,1)}), bf16[64,3,2048]{2,1,0:T(4,128)(2,1)}, u32[]{:S(2)}, u32[]{:S(2)}) async-start(bf16[64,3,2048]{2,1,0:T(4,128)(2,1)} %reshape.660), calls=%async_computation.28 | async-start | bytes 2097152 | tf_op jit(solution)/shard_map/all_to_all | solution.py:62
  1000.1 9.3 collective-permute-start.9
  1012.4 36.3 %all-to-all-start.29 = ((bf16[64,3,2048]{2,1,0:T(4,128)(2,1)}), bf16[64,3,2048]{2,1,0:T(4,128)(2,1)}, u32[]{:S(2)}, u32[]{:S(2)}) async-start(bf16[64,3,2048]{2,1,0:T(4,128)(2,1)} %copy.257), calls=%async_computation.29 | async-start | bytes 2097152 | tf_op jit(solution)/shard_map/all_to_all | solution.py:58
  1058.4 8.4 copy-start.16
  1058.4 8.5 copy-start.27
  1061.6 24.4 %all-to-all-start.30 = ((bf16[64,3,2048]{2,1,0:T(4,128)(2,1)}), bf16[64,3,2048]{2,1,0:T(4,128)(2,1)}, u32[]{:S(2)}, u32[]{:S(2)}) async-start(bf16[64,3,2048]{2,1,0:T(4,128)(2,1)} %reshape.662), calls=%async_computation.30 | async-start | bytes 2097152 | tf_op jit(solution)/shard_map/all_to_all | solution.py:62
  1090.1 24.7 %collective-permute-start.10 = (bf16[32,2048]{1,0:T(8,128)(2,1)S(1)}, bf16[32,2048]{1,0:T(8,128)(2,1)S(1)}, u32[]{:S(2)}, u32[]{:S(2)}) collective-permute-start(bf16[32,2048]{1,0:T(8,128)(2,1)S(1)} %get-tuple-element.782), channel_id=1, source_target_pairs={{8,0},{16,8},{24,16},{9,1},{17,9},{25,17},{10,2},{18,10},{26,18},{... | collective-permute-start | bytes 393224 | tf_op jit(solution)/shard_map/ppermute | solution.py:15
  1117.9 33.7 %all-to-all-start.31 = ((bf16[64,3,2048]{2,1,0:T(4,128)(2,1)}), bf16[64,3,2048]{2,1,0:T(4,128)(2,1)}, u32[]{:S(2)}, u32[]{:S(2)}) async-start(bf16[64,3,2048]{2,1,0:T(4,128)(2,1)} %copy.259), calls=%async_computation.31 | async-start | bytes 2097152 | tf_op jit(solution)/shard_map/all_to_all | solution.py:58
  1161.3 8.8 copy-start.15
  1161.3 8.9 copy-start.26
  1164.6 33.5 %all-to-all-start.32 = ((bf16[64,3,2048]{2,1,0:T(4,128)(2,1)}), bf16[64,3,2048]{2,1,0:T(4,128)(2,1)}, u32[]{:S(2)}, u32[]{:S(2)}) async-start(bf16[64,3,2048]{2,1,0:T(4,128)(2,1)} %reshape.664), calls=%async_computation.32 | async-start | bytes 2097152 | tf_op jit(solution)/shard_map/all_to_all | solution.py:62
  1202.1 6.4 collective-permute-start.11
  1211.5 31.9 %all-to-all-start.33 = ((bf16[64,3,2048]{2,1,0:T(4,128)(2,1)}), bf16[64,3,2048]{2,1,0:T(4,128)(2,1)}, u32[]{:S(2)}, u32[]{:S(2)}) async-start(bf16[64,3,2048]{2,1,0:T(4,128)(2,1)} %copy.261), calls=%async_computation.33 | async-start | bytes 2097152 | tf_op jit(solution)/shard_map/all_to_all | solution.py:58
  1243.3 29.7 %all-to-all-start.20 = ((bf16[64,3,2048]{2,1,0:T(4,128)(2,1)}), bf16[64,3,2048]{2,1,0:T(4,128)(2,1)}, u32[]{:S(2)}, u32[]{:S(2)}) async-start(bf16[64,3,2048]{2,1,0:T(4,128)(2,1)} %reshape.651), calls=%async_computation.20 | async-start | bytes 2097152 | tf_op jit(solution)/shard_map/all_to_all | solution.py:54
  1261.1 17.2 %copy-start.6 = (bf16[5,32,2048]{2,1,0:T(8,128)(2,1)S(1)}, bf16[5,32,2048]{2,1,0:T(8,128)(2,1)}, u32[]{:S(2)}) copy-start(bf16[5,32,2048]{2,1,0:T(8,128)(2,1)} %get-tuple-element.848) | copy-start | bytes 1966084
  1273.1 27.2 %all-to-all-start.34 = ((bf16[64,3,2048]{2,1,0:T(4,128)(2,1)}), bf16[64,3,2048]{2,1,0:T(4,128)(2,1)S(1)}, u32[]{:S(2)}, u32[]{:S(2)}) async-start(bf16[64,3,2048]{2,1,0:T(4,128)(2,1)} %reshape.666), calls=%async_computation.34 | async-start | bytes 2097152 | tf_op jit(solution)/shard_map/all_to_all | solution.py:62
  1278.3 227.0 %copy-start.4 = (bf16[5,32,2048]{2,1,0:T(8,128)(2,1)S(1)}, bf16[5,32,2048]{2,1,0:T(8,128)(2,1)}, u32[]{:S(2)}) copy-start(bf16[5,32,2048]{2,1,0:T(8,128)(2,1)} %get-tuple-element.779) | copy-start | bytes 1966084
  (11 other events, 21.7 us)
where the time goes:
time: 1520 us; the launch traced here: 1510 us
  waiting for transfers between devices  747 us (49%)
  starting transfers between devices  290 us (19%)
  blocking collectives  203 us (13%)
  local copies, waits for them, and re-layouts  141 us (9%)
  matrix products  92.5 us (6%)
  other arithmetic  31.6 us (2%)
    psum x1, blocking collectives, body(): gain_grad = lax.psum(gain_sum, ('dp', 'expert'))  203 us
    all_to_all x7, waiting for transfers between devices, send_rows(): lax.all_to_all(row_block, ('dp', 'expert'), split_axis=0, concat_axis=0,...  177 us
    all_to_all x7, waiting for transfers between devices, send_grads(): lax.all_to_all(row_block, ('dp', 'expert'), split_axis=0, concat_axis=0,...  165 us
    all_to_all x7, waiting for transfers between devices, return_grads(): lax.all_to_all(row_block, ('dp', 'expert'), split_axis=0, concat_axis=0,...  144 us
    all_to_all x7, waiting for transfers between devices, return_rows(): lax.all_to_all(row_block, ('dp', 'expert'), split_axis=0, concat_axis=0,...  138 us
    ppermute x12, waiting for transfers between devices, from_behind(): lax.ppermute(value, axis, [(source, source + steps) for source in range(l...  79.9 us
    all_to_all x7, starting transfers between devices, send_rows(): lax.all_to_all(pair_block, ('dp', 'expert'), split_axis=0, concat_axis=0,...  58 us
    all_to_all x7, starting transfers between devices, send_grads(): lax.all_to_all(row_block, ('dp', 'expert'), split_axis=0, concat_axis=0,...  54.3 us
  transfers between devices with their start and end apart: 47, of which 41 were waited for; matrix products, arithmetic and copies ran while one was open for 5% of the time, Pallas kernels for 0%

commit v1 on v0

v1 whole, which is shorter than its diff:
```python
import jax
import jax.numpy as jnp
from jax import lax
from jax.experimental import pallas as pl
from jax.experimental.pallas import tpu as pltpu
from jax.sharding import PartitionSpec as P

MICRO = 4
ROWS = 32
CAP = 3
CHUNKS = 4
EXTRA = 128
EPS = 1e-06
MESH = pl.DeviceIdType.MESH
F32 = jnp.float32
BF16 = jnp.bfloat16


def dot(a, b):
    return jnp.dot(a, b, preferred_element_type=F32)


def dot_last(a, b):
    return lax.dot_general(a, b, (((1,), (1,)), ((), ())), preferred_element_type=F32)


def dot_first(a, b):
    return lax.dot_general(a, b, (((0,), (0,)), ((), ())), preferred_element_type=F32)


def kernel(
    tokens, cotangent, ids, gates, gain, w_gate, w_up, w_down,
    seg_out, seg_grad, gain_out,
    mats, down, cw_own, cw_par, cw_send,
    xa, xb, outs, part, szs, szr, dsend, drec, rsend, rrec, keep, ssq, hid, grad_in, gacc, grec, gtot, gpar,
    s_in_a, s_in_b, s_drec, s_rrec, s_szr, s_dsend, s_rsend, s_szs, s_pga, s_pgb, s_load, s_cw, s_out, s_g,
):
    dp, stage, ex = lax.axis_index("dp"), lax.axis_index("pipe"), lax.axis_index("expert")
    half, xpos = lax.rem(dp, 2), dp // 2
    n_ex = lax.axis_size("expert")
    stages = lax.axis_size("pipe")
    peers = lax.axis_size("dp") * n_ex // 2
    slots = peers * 8
    width = down.shape[1]
    hidden = down.shape[0]
    cw = width // CHUNKS
    me = xpos * n_ex + ex

    def plane(d):
        return (2 * (d // n_ex) + half, stage, lax.rem(d, n_ex))

    partner = (2 * xpos + 1 - half, stage, ex)

    def same(st):
        return (dp, st, ex)

    def other(st):
        return (2 * xpos + 1 - half, st, ex)

    load = [
        pltpu.make_async_copy(w_gate.at[0, 0], mats.at[:, pl.ds(0, hidden)], s_load.at[0]),
        pltpu.make_async_copy(w_up.at[0, 0], mats.at[:, pl.ds(hidden, hidden)], s_load.at[1]),
        pltpu.make_async_copy(w_down.at[0, 0], down, s_load.at[2]),
    ]
    for c in load:
        c.start()

    bar = pltpu.get_barrier_semaphore()

    def greet(dev):
        pl.semaphore_signal(bar, inc=1, device_id=dev, device_id_type=MESH)

    @pl.loop(1, peers)
    def _(i):
        greet(plane(lax.rem(me + i, peers)))

    greet(partner)

    @pl.when(stage > 0)
    def _():
        greet(same(stage - 1))
        greet(other(stage - 1))

    @pl.when(stage < stages - 1)
    def _():
        greet(same(stage + 1))
        greet(other(stage + 1))

    rows = MICRO * ROWS
    n_own = 2 * peers
    lane_o = lax.broadcasted_iota(jnp.int32, (rows, n_own), 1)
    idv = ids[0]
    gv = gates[0].astype(F32)
    member = jnp.zeros((rows, n_own), F32)
    chosen = jnp.zeros((rows, n_own), F32)
    for j in range(idv.shape[1]):
        hit = idv[:, j : j + 1] == lane_o
        member = member + jnp.where(hit, 1.0, 0.0)
        chosen = chosen + jnp.where(hit, gv[:, j : j + 1], 0.0)
    ri = lax.broadcasted_iota(jnp.int32, (rows, rows), 0)
    ci = lax.broadcasted_iota(jnp.int32, (rows, rows), 1)
    earlier = jnp.where((ci < ri) & (ci // ROWS == ri // ROWS), 1.0, 0.0).astype(BF16)
    member = member.astype(BF16)
    position = dot(earlier, member).astype(BF16)
    chosen = chosen.astype(BF16)
    oi = lax.broadcasted_iota(jnp.int32, (n_own, slots), 0)
    si = lax.broadcasted_iota(jnp.int32, (n_own, slots), 1) // 8
    kk = lax.broadcasted_iota(jnp.int32, (rows, slots), 1) % 8

    def table(plane_half, first):
        owner = (2 * (si // n_ex) + plane_half) * n_ex + si % n_ex
        spread = jnp.where(oi == owner, 1.0, 0.0).astype(BF16)
        pos = dot(position, spread)
        wts = dot(chosen, spread)
        return jnp.where(pos == (kk - first).astype(F32), wts, 0.0).astype(BF16)

    cw_own[...] = table(half, 0)
    cw_send[...] = table(1 - half, CAP)
    gacc[...] = jnp.zeros_like(gacc)

    mates = 2 * jnp.where(stage > 0, 1, 0) + 2 * jnp.where(stage < stages - 1, 1, 0)
    pl.semaphore_wait(bar, peers + mates)

    cw_copy = pltpu.make_async_remote_copy(
        cw_send, cw_par, s_cw.at[0], s_cw.at[1], device_id=partner, device_id_type=MESH
    )
    cw_copy.start()

    def cols(k):
        return pl.ds(k * cw, cw)

    def rcols(k, extra):
        if k == 0 and extra:
            return pl.ds(0, EXTRA + cw)
        return pl.ds(EXTRA + k * cw, cw)

    def feed(src, base):
        @pl.loop(0, MICRO)
        def _(m):
            q = base + m
            r = pl.ds(pl.multiple_of(m * ROWS, ROWS), ROWS)
            for k in range(CHUNKS):
                pltpu.make_async_copy(
                    src.at[r, cols(k)], xa.at[q, :, cols(k)], s_in_a.at[q * CHUNKS + k]
                ).start()
                pltpu.make_async_remote_copy(
                    src.at[r, cols(k)], xb.at[q, :, cols(k)], s_g.at[2],
                    s_in_b.at[q * CHUNKS + k], device_id=partner, device_id_type=MESH,
                ).start()

    @pl.when(stage == 0)
    def _():
        feed(tokens, 0)

    for c in load:
        c.wait()
    step = 256

    @pl.loop(0, width // step)
    def _(i):
        r = pl.ds(pl.multiple_of(i * step, step), step)
        mats[r, :] = (mats[r, :].astype(F32) * gain[r, :]).astype(BF16)

    cw_copy.wait()

    def fan_out(send, rec, q, sl, s_send, s_rec):
        pltpu.make_async_copy(send.at[me, pl.ds(0, 2 * CAP), sl], rec.at[q, me, pl.ds(0, 2 * CAP), sl], s_rec).start()

        @pl.loop(1, peers)
        def _(i):
            d = lax.rem(me + i, peers)
            pltpu.make_async_remote_copy(
                send.at[d, pl.ds(0, 2 * CAP), sl], rec.at[q, me, pl.ds(0, 2 * CAP), sl],
                s_send, s_rec, device_id=plane(d), device_id_type=MESH,
            ).start()

    def wait_all(ref, sem):
        pltpu.make_async_copy(ref, ref, sem).wait()

    def section(m, back):
        q = m + (MICRO if back else 0)
        mrow = pl.ds(pl.multiple_of(m * ROWS, ROWS), ROWS)
        both = jnp.concatenate([cw_own[mrow, :], cw_par[mrow, :]], axis=0)
        place = jnp.where(both > 0, 1.0, 0.0).astype(BF16)
        for k in range(CHUNKS):
            i = q * CHUNKS + k
            wait_all(xa.at[q, :, cols(k)], s_in_a.at[i])
            wait_all(xb.at[q, :, cols(k)], s_in_b.at[i])
            src = jnp.concatenate([xa[q, :, cols(k)], xb[q, :, cols(k)]], axis=0)
            dsend[:, :, cols(k)] = dot_first(place, src).astype(BF16).reshape(peers, 8, cw)
            fan_out(dsend, drec, q, cols(k), s_dsend, s_drec.at[i])
        for k in range(CHUNKS):
            i = q * CHUNKS + k
            wait_all(drec.at[q, :, pl.ds(0, 2 * CAP), cols(k)], s_drec.at[i])
            got = drec[q, :, :, cols(k)].reshape(slots, cw)
            if back:
                term = dot_last(got, down[:, cols(k)])
                if k == 0:
                    grad_in[...] = term
                else:
                    grad_in[...] += term
            else:
                term = dot(got, mats[cols(k), :])
                gf = got.astype(F32)
                gf = gf * gf
                sq = gf[:, :128]
                for j in range(1, cw // 128):
                    sq = sq + gf[:, j * 128 : (j + 1) * 128]
                if k == 0:
                    keep[m] = term
                    ssq[...] = sq
                else:
                    keep[m] += term
                    ssq[...] += sq
        if back:
            gp, up = keep[m, :, :hidden], keep[m, :, hidden:]
            qv = grad_in[...]
            sg = jax.nn.sigmoid(gp)
            dg = (qv * up * sg * (1.0 + gp * (1.0 - sg))).astype(BF16)
            du = (qv * gp * sg).astype(BF16)
            hid[:, :hidden] = dg
            hid[:, hidden:] = du
            kap = jnp.sum(dg.astype(F32) * gp + du.astype(F32) * up, axis=1, keepdims=True)
            rsend[:, :, :EXTRA] = jnp.broadcast_to(kap, (slots, EXTRA)).astype(BF16).reshape(peers, 8, EXTRA)
        else:
            scale = lax.rsqrt(jnp.sum(ssq[...], axis=1, keepdims=True) / width + EPS)
            pre = keep[m] * scale
            keep[m] = pre
            gp, up = pre[:, :hidden], pre[:, hidden:]
            hid[:, :hidden] = (gp * jax.nn.sigmoid(gp) * up).astype(BF16)
        for k in range(CHUNKS):
            if back:
                res = dot_last(hid[...], mats[cols(k), :])
            else:
                res = dot(hid[:, :hidden], down[:, cols(k)])
            rsend[:, :, pl.ds(EXTRA + k * cw, cw)] = res.astype(BF16).reshape(peers, 8, cw)
            fan_out(rsend, rrec, q, rcols(k, back), s_rsend, s_rrec.at[q * CHUNKS + k])
        if back:
            xf = xa[m].astype(F32)
            sc = lax.rsqrt(jnp.sum(xf * xf, axis=1, keepdims=True) / width + EPS)
        coef = None
        kap_own = None
        live = lax.broadcasted_iota(jnp.int32, (peers, 8, cw), 1) < 2 * CAP
        for k in range(CHUNKS + 1):
            if k < CHUNKS:
                i = q * CHUNKS + k
                wait_all(rrec.at[q, :, pl.ds(0, 2 * CAP), rcols(k, back)], s_rrec.at[i])
                got = rrec[q, :, :, pl.ds(EXTRA + k * cw, cw)]
                got = jnp.where(live, got, jnp.zeros_like(got)).reshape(slots, cw)
                term = dot(both, got)
                part[:, cols(k)] = term[:ROWS]
                szs[q, :, pl.ds(EXTRA + k * cw, cw)] = term[ROWS:].astype(BF16)
                if back and k == 0:
                    kr = rrec[q, :, :, :EXTRA]
                    kr = jnp.where(live[:, :, :EXTRA], kr, jnp.zeros_like(kr)).reshape(slots, EXTRA)
                    kt = dot(both, kr)
                    kap_own = kt[:ROWS]
                    szs[q, :, :EXTRA] = kt[ROWS:].astype(BF16)
                pltpu.make_async_remote_copy(
                    szs.at[q, :, rcols(k, back)], szr.at[q, :, rcols(k, back)], s_szs,
                    s_szr.at[i], device_id=partner, device_id_type=MESH,
                ).start()
            if k > 0:
                j = k - 1
                i = q * CHUNKS + j
                wait_all(szr.at[q, :, rcols(j, back)], s_szr.at[i])
                add = part[:, cols(j)] + szr[q, :, pl.ds(EXTRA + j * cw, cw)].astype(F32)
                base = xa[q, :, cols(j)].astype(F32)
                if back:
                    if j == 0:
                        kap_all = (kap_own + szr[q, :, :EXTRA].astype(F32))[:, :1]
                        coef = sc * sc * kap_all / width
                    xj = xa[m, :, cols(j)].astype(F32)
                    gacc[:, cols(j)] += jnp.sum(add * xj * sc, axis=0, keepdims=True)
                    res = base + sc * add - xj * coef
                else:
                    res = base + add
                outs[q, :, cols(j)] = res.astype(BF16)

                def pass_on(st):
                    pltpu.make_async_remote_copy(
                        outs.at[q, :, cols(j)], xa.at[q, :, cols(j)], s_pga,
                        s_in_a.at[i], device_id=same(st), device_id_type=MESH,
                    ).start()
                    pltpu.make_async_remote_copy(
                        outs.at[q, :, cols(j)], xb.at[q, :, cols(j)], s_pgb,
                        s_in_b.at[i], device_id=other(st), device_id_type=MESH,
                    ).start()

                if back:

                    @pl.when(stage > 0)
                    def _():
                        pass_on(stage - 1)
                else:

                    @pl.when(stage < stages - 1)
                    def _():
                        pass_on(stage + 1)

        target = seg_grad if back else seg_out
        pltpu.make_async_copy(outs.at[q], target.at[0, mrow, :], s_out.at[q]).start()
        wait_all(dsend.at[pl.ds(0, peers - 1), pl.ds(0, 2 * CAP), :], s_dsend)
        if back:
            wait_all(rsend.at[pl.ds(0, peers - 1), pl.ds(0, 2 * CAP), :], s_rsend)
            wait_all(szs.at[q], s_szs)
        else:
            wait_all(rsend.at[pl.ds(0, peers - 1), pl.ds(0, 2 * CAP), pl.ds(EXTRA, width)], s_rsend)
            wait_all(szs.at[q, :, pl.ds(EXTRA, width)], s_szs)
        passes = (stage > 0) if back else (stage < stages - 1)

        @pl.when(passes)
        def _():
            wait_all(outs.at[q], s_pga)
            wait_all(outs.at[q], s_pgb)

    @pl.loop(0, MICRO)
    def _(m):
        section(m, False)

    @pl.when(stage == stages - 1)
    def _():
        feed(cotangent, MICRO)

    @pl.loop(0, MICRO)
    def _(m):
        section(m, True)

    grec[me] = gacc[...]

    @pl.loop(1, peers)
    def _(i):
        d = lax.rem(me + i, peers)
        pltpu.make_async_remote_copy(
            gacc, grec.at[me], s_g.at[0], s_g.at[1], device_id=plane(d), device_id_type=MESH
        ).start()

    wait_all(grec.at[pl.ds(0, peers - 1)], s_g.at[1])
    wait_all(grec.at[pl.ds(0, peers - 1)], s_g.at[0])
    gtot[...] = jnp.sum(grec[...], axis=0)
    last = pltpu.make_async_remote_copy(
        gtot, gpar, s_g.at[3], s_g.at[4], device_id=partner, device_id_type=MESH
    )
    last.start()
    last.wait()
    gain_out[...] = gtot[...] + gpar[...]

    @pl.when(stage == 0)
    def _():
        wait_all(tokens, s_g.at[2])

    @pl.when(stage == stages - 1)
    def _():
        wait_all(cotangent, s_g.at[2])

    @pl.loop(0, 2 * MICRO)
    def _(q):
        wait_all(outs.at[q], s_out.at[q])


def body(tokens, cotangent, owner_ids, gate_weights, norm_gain, w_gate, w_up, w_down):
    width = tokens.shape[1]
    hidden = w_down.shape[2]
    peers = lax.axis_size("dp") * lax.axis_size("expert") // 2
    slots = peers * 8
    rows = MICRO * ROWS
    wide = EXTRA + width
    gain_col = norm_gain.reshape(width, 1)
    hbm = pl.BlockSpec(memory_space=pl.ANY)
    vmem = pl.BlockSpec(memory_space=pltpu.VMEM)
    dma = pltpu.SemaphoreType.DMA
    seg_out, seg_grad, weighted = pl.pallas_call(
        kernel,
        out_shape=(
            jax.ShapeDtypeStruct((1, rows, width), BF16),
            jax.ShapeDtypeStruct((1, rows, width), BF16),
            jax.ShapeDtypeStruct((1, width), F32),
        ),
        in_specs=[hbm, hbm, vmem, vmem, vmem, hbm, hbm, hbm],
        out_specs=(hbm, hbm, vmem),
        scratch_shapes=[
            pltpu.VMEM((width, 2 * hidden), BF16),
            pltpu.VMEM((hidden, width), BF16),
            pltpu.VMEM((rows, slots), BF16),
            pltpu.VMEM((rows, slots), BF16),
            pltpu.VMEM((rows, slots), BF16),
            pltpu.VMEM((2 * MICRO, ROWS, width), BF16),
            pltpu.VMEM((2 * MICRO, ROWS, width), BF16),
            pltpu.VMEM((2 * MICRO, ROWS, width), BF16),
            pltpu.VMEM((ROWS, width), F32),
            pltpu.VMEM((2 * MICRO, ROWS, wide), BF16),
            pltpu.VMEM((2 * MICRO, ROWS, wide), BF16),
            pltpu.VMEM((peers, 8, width), BF16),
            pltpu.VMEM((2 * MICRO, peers, 8, width), BF16),
            pltpu.VMEM((peers, 8, wide), BF16),
            pltpu.VMEM((2 * MICRO, peers, 8, wide), BF16),
            pltpu.VMEM((MICRO, slots, 2 * hidden), F32),
            pltpu.VMEM((slots, 128), F32),
            pltpu.VMEM((slots, 2 * hidden), BF16),
            pltpu.VMEM((slots, hidden), F32),
            pltpu.VMEM((1, width), F32),
            pltpu.VMEM((peers, 1, width), F32),
            pltpu.VMEM((1, width), F32),
            pltpu.VMEM((1, width), F32),
            dma((2 * MICRO * CHUNKS,)),
            dma((2 * MICRO * CHUNKS,)),
            dma((2 * MICRO * CHUNKS,)),
            dma((2 * MICRO * CHUNKS,)),
            dma((2 * MICRO * CHUNKS,)),
            dma,
            dma,
            dma,
            dma,
            dma,
            dma((3,)),
            dma((2,)),
            dma((2 * MICRO,)),
            dma((5,)),
        ],
        compiler_params=pltpu.CompilerParams(
            collective_id=0, has_side_effects=True, vmem_limit_bytes=56 << 20
        ),
        name="relay",
    )(tokens, cotangent, owner_ids, gate_weights, gain_col, w_gate, w_up, w_down)
    return (seg_out, seg_grad, weighted / norm_gain)


def solution(mesh):
    in_specs = (
        P(("dp", "expert"), None),
        P(("dp", "expert"), None),
        P("pipe", ("dp", "expert"), None),
        P("pipe", ("dp", "expert"), None),
        P("pipe", None),
        P("pipe", ("dp", "expert"), None, None),
        P("pipe", ("dp", "expert"), None, None),
        P("pipe", ("dp", "expert"), None, None),
    )
    out_specs = (
        P("pipe", ("dp", "expert"), None),
        P("pipe", ("dp", "expert"), None),
        P("pipe", None),
    )
    return jax.shard_map(body, mesh=mesh, in_specs=in_specs, out_specs=out_specs, check_vma=False)
```

time: 1520 us -> 501 us (0.33)
  waiting for transfers between devices: 747 us -> 0 us
  Pallas kernels: 0 us -> 490 us
  starting transfers between devices: 290 us -> 0 us
  blocking collectives: 203 us -> 0 us
  local copies, waits for them, and re-layouts: 141 us -> 8.63 us
  matrix products: 92.5 us -> 0 us
  other arithmetic: 31.6 us -> 1.31 us
    all_to_all x35 -> x0, waiting for transfers between devices: 667 us -> none  [the longest x7 177 us: send_rows(): lax.all_to_all(row_block, ('dp', 'expert'), split_axis=0, concat_axis=0,...]
    pallas_call x0 -> x1, Pallas kernels: none -> 490 us  [body(): pl.pallas_call(kernel, out_shape=(jax.ShapeDtypeStruct((1, rows, width),...]
    all_to_all x35 -> x0, starting transfers between devices: 249 us -> none  [the longest x7 58 us: send_rows(): lax.all_to_all(pair_block, ('dp', 'expert'), split_axis=0, concat_axis=0,...]
    psum x1 -> x0, blocking collectives: 203 us -> none  [body(): gain_grad = lax.psum(gain_sum, ('dp', 'expert'))]
    dot_general x51 -> x0, matrix products: 92.5 us -> none  [the longest x7 18.9 us: body(): jnp.einsum('okr,okd->rd', f_placing, returned, preferred_element_type=jnp...]
    ppermute x12 -> x0, waiting for transfers between devices: 79.9 us -> none  [from_behind(): lax.ppermute(value, axis, [(source, source + steps) for source in range(l...]
    reshape x22 -> x1, local copies, waits for them, and re-layouts: 71.5 us -> 2.04 us  [body(): gain_col = norm_gain.reshape(width, 1)]
    ppermute x12 -> x0, starting transfers between devices: 40.4 us -> none  [from_behind(): lax.ppermute(value, axis, [(source, source + steps) for source in range(l...]
  transfers between devices with their start and end apart: 47 -> 0, of which waited for: 41 -> 0; matrix products, arithmetic and copies ran while one was open for 5% -> 0% of each run, Pallas kernels for 0% -> 0%
where the time goes in v1:
time: 501 us
  Pallas kernels  490 us (98%)
  local copies, waits for them, and re-layouts  8.63 us (2%)
    pallas_call x1, Pallas kernels, body(): pl.pallas_call(kernel, out_shape=(jax.ShapeDtypeStruct((1, rows, width),...  490 us

profile of v1, /device:TPU:1, one launch (start us, length us, event | category | flops | bytes accessed | tf_op | source)
XLA Modules:
  0.0 500.6 jit_solution(12959841369772585658)
XLA Ops:
  0.6 1.4 copy.14.gates
  2.0 1.4 copy.13.ids
  3.5 2.0 copy.15.gain
  5.5 0.0 copy-start
  5.5 490.0 %relay.1 = (bf16[1,128,2048]{2,1,0:T(8,128)(2,1)}, bf16[1,128,2048]{2,1,0:T(8,128)(2,1)}, f32[1,2048]{1,0:T(1,128)}) custom-call(bf16[128,2048]{1,0:T(8,128)(2,1)} %tokens.1, bf16[128,2048]{1,0:T(8,128)(2,1)} %cotangent.1, s32[1,128,4]{2,1,0:T(8,128)} %copy.13.ids, bf16[1,128,4]{2,1,0:T(8,128)(2,1)} %copy.14.gates, f32[2048,1]{1,0:T(8,128)} %copy.15.gain, ...), custom_call_target="tpu_custom_call" | custom-call | tf_op jit(solution)/shard_map/relay/pallas_call | solution.py:372
  495.5 0.0 copy-done
  495.5 1.3 div.3
  496.8 1.9 copy.18
  498.7 1.9 copy.19
Async XLA Ops:
  5.5 490.0 %copy-start = (f32[1,2048]{1,0:T(1,128)S(1)}, f32[1,2048]{1,0:T(1,128)}, u32[]{:S(2)}) copy-start(f32[1,2048]{1,0:T(1,128)} %param.12) | copy-start | bytes 24580

commit v2 on v1

--- a/solution.py
+++ b/solution.py
@@ -8,7 +8,9 @@
 MICRO = 4
 ROWS = 32
 CAP = 3
-CHUNKS = 4
+WIDTHS = (6, 6, 4)
+CHUNKS = len(WIDTHS)
+ORDER = "CDDCDC"
 EXTRA = 128
 EPS = 1e-06
 MESH = pl.DeviceIdType.MESH
@@ -30,7 +32,7 @@
 
 def kernel(
     tokens, cotangent, ids, gates, gain, w_gate, w_up, w_down,
-    seg_out, seg_grad, gain_out,
+    seg_both, gain_out,
     mats, down, cw_own, cw_par, cw_send,
     xa, xb, outs, part, szs, szr, dsend, drec, rsend, rrec, keep, ssq, hid, grad_in, gacc, grec, gtot, gpar,
     s_in_a, s_in_b, s_drec, s_rrec, s_szr, s_dsend, s_rsend, s_szs, s_pga, s_pgb, s_load, s_cw, s_out, s_g,
@@ -43,8 +45,10 @@
     slots = peers * 8
     width = down.shape[1]
     hidden = down.shape[0]
-    cw = width // CHUNKS
+    cws = [w * width // 16 for w in WIDTHS]
+    starts = [sum(cws[:k]) for k in range(CHUNKS)]
     me = xpos * n_ex + ex
+    ex_at = [lax.rem(ex + i, n_ex) for i in range(n_ex)]
 
     def plane(d):
         return (2 * (d // n_ex) + half, stage, lax.rem(d, n_ex))
@@ -88,20 +92,20 @@
 
     rows = MICRO * ROWS
     n_own = 2 * peers
-    lane_o = lax.broadcasted_iota(jnp.int32, (rows, n_own), 1)
+    row_o = lax.broadcasted_iota(jnp.int32, (n_own, rows), 0)
     idv = ids[0]
     gv = gates[0].astype(F32)
-    member = jnp.zeros((rows, n_own), F32)
-    chosen = jnp.zeros((rows, n_own), F32)
-    for j in range(idv.shape[1]):
-        hit = idv[:, j : j + 1] == lane_o
+    member = jnp.zeros((n_own, rows), F32)
+    chosen = jnp.zeros((n_own, rows), F32)
+    for j in range(idv.shape[0]):
+        hit = idv[j : j + 1, :] == row_o
         member = member + jnp.where(hit, 1.0, 0.0)
-        chosen = chosen + jnp.where(hit, gv[:, j : j + 1], 0.0)
+        chosen = chosen + jnp.where(hit, gv[j : j + 1, :], 0.0)
     ri = lax.broadcasted_iota(jnp.int32, (rows, rows), 0)
     ci = lax.broadcasted_iota(jnp.int32, (rows, rows), 1)
-    earlier = jnp.where((ci < ri) & (ci // ROWS == ri // ROWS), 1.0, 0.0).astype(BF16)
+    earlier = jnp.where((ri < ci) & (ci // ROWS == ri // ROWS), 1.0, 0.0).astype(BF16)
     member = member.astype(BF16)
-    position = dot(earlier, member).astype(BF16)
+    position = dot(member, earlier).astype(BF16)
     chosen = chosen.astype(BF16)
     oi = lax.broadcasted_iota(jnp.int32, (n_own, slots), 0)
     si = lax.broadcasted_iota(jnp.int32, (n_own, slots), 1) // 8
@@ -110,8 +114,8 @@
     def table(plane_half, first):
         owner = (2 * (si // n_ex) + plane_half) * n_ex + si % n_ex
         spread = jnp.where(oi == owner, 1.0, 0.0).astype(BF16)
-        pos = dot(position, spread)
-        wts = dot(chosen, spread)
+        pos = dot_first(position, spread)
+        wts = dot_first(chosen, spread)
         return jnp.where(pos == (kk - first).astype(F32), wts, 0.0).astype(BF16)
 
     cw_own[...] = table(half, 0)
@@ -127,12 +131,15 @@
     cw_copy.start()
 
     def cols(k):
-        return pl.ds(k * cw, cw)
+        return pl.ds(starts[k], cws[k])
+
+    def rdata(k):
+        return pl.ds(EXTRA + starts[k], cws[k])
 
     def rcols(k, extra):
         if k == 0 and extra:
-            return pl.ds(0, EXTRA + cw)
-        return pl.ds(EXTRA + k * cw, cw)
+            return pl.ds(0, EXTRA + cws[0])
+        return rdata(k)
 
     def feed(src, base):
         @pl.loop(0, MICRO)
@@ -152,47 +159,60 @@
     def _():
         feed(tokens, 0)
 
-    for c in load:
-        c.wait()
-    step = 256
-
-    @pl.loop(0, width // step)
-    def _(i):
-        r = pl.ds(pl.multiple_of(i * step, step), step)
-        mats[r, :] = (mats[r, :].astype(F32) * gain[r, :]).astype(BF16)
-
     cw_copy.wait()
 
     def fan_out(send, rec, q, sl, s_send, s_rec):
         pltpu.make_async_copy(send.at[me, pl.ds(0, 2 * CAP), sl], rec.at[q, me, pl.ds(0, 2 * CAP), sl], s_rec).start()
 
-        @pl.loop(1, peers)
-        def _(i):
-            d = lax.rem(me + i, peers)
-            pltpu.make_async_remote_copy(
-                send.at[d, pl.ds(0, 2 * CAP), sl], rec.at[q, me, pl.ds(0, 2 * CAP), sl],
-                s_send, s_rec, device_id=plane(d), device_id_type=MESH,
-            ).start()
+        def to_row(dx, first):
+            x = lax.rem(xpos + dx, peers // n_ex)
+            for de in range(first, n_ex):
+                e = ex_at[de]
+                d = x * n_ex + e
+                pltpu.make_async_remote_copy(
+                    send.at[d, pl.ds(0, 2 * CAP), sl], rec.at[q, me, pl.ds(0, 2 * CAP), sl],
+                    s_send, s_rec, device_id=(2 * x + half, stage, e), device_id_type=MESH,
+                ).start()
+
+        to_row(0, 1)
+
+        @pl.loop(1, peers // n_ex)
+        def _(dx):
+            to_row(dx, 0)
 
     def wait_all(ref, sem):
         pltpu.make_async_copy(ref, ref, sem).wait()
 
-    def section(m, back):
+    def tables(m):
+        mrow = pl.ds(pl.multiple_of(m * ROWS, ROWS), ROWS)
+        return jnp.concatenate([cw_own[mrow, :], cw_par[mrow, :]], axis=0)
+
+    def dispatch(m, back, prior):
         q = m + (MICRO if back else 0)
-        mrow = pl.ds(pl.multiple_of(m * ROWS, ROWS), ROWS)
-        both = jnp.concatenate([cw_own[mrow, :], cw_par[mrow, :]], axis=0)
-        place = jnp.where(both > 0, 1.0, 0.0).astype(BF16)
+        place = jnp.where(tables(m) > 0, 1.0, 0.0).astype(BF16)
         for k in range(CHUNKS):
             i = q * CHUNKS + k
             wait_all(xa.at[q, :, cols(k)], s_in_a.at[i])
             wait_all(xb.at[q, :, cols(k)], s_in_b.at[i])
+            if k == 0 and prior:
+                wait_all(dsend.at[pl.ds(0, peers - 1), pl.ds(0, 2 * CAP), :], s_dsend)
             src = jnp.concatenate([xa[q, :, cols(k)], xb[q, :, cols(k)]], axis=0)
-            dsend[:, :, cols(k)] = dot_first(place, src).astype(BF16).reshape(peers, 8, cw)
+            dsend[:, :, cols(k)] = dot_first(place, src).astype(BF16).reshape(peers, 8, cws[k])
             fan_out(dsend, drec, q, cols(k), s_dsend, s_drec.at[i])
+            yield
+
+    def sent_back(back):
+        if back:
+            wait_all(rsend.at[pl.ds(0, peers - 1), pl.ds(0, 2 * CAP), :], s_rsend)
+        else:
+            wait_all(rsend.at[pl.ds(0, peers - 1), pl.ds(0, 2 * CAP), pl.ds(EXTRA, width)], s_rsend)
+
+    def expert(m, back, prior):
+        q = m + (MICRO if back else 0)
         for k in range(CHUNKS):
             i = q * CHUNKS + k
             wait_all(drec.at[q, :, pl.ds(0, 2 * CAP), cols(k)], s_drec.at[i])
-            got = drec[q, :, :, cols(k)].reshape(slots, cw)
+            got = drec[q, :, :, cols(k)].reshape(slots, cws[k])
             if back:
                 term = dot_last(got, down[:, cols(k)])
                 if k == 0:
@@ -204,7 +224,7 @@
                 gf = got.astype(F32)
                 gf = gf * gf
                 sq = gf[:, :128]
-                for j in range(1, cw // 128):
+                for j in range(1, cws[k] // 128):
                     sq = sq + gf[:, j * 128 : (j + 1) * 128]
                 if k == 0:
                     keep[m] = term
@@ -212,6 +232,8 @@
                 else:
                     keep[m] += term
                     ssq[...] += sq
+        if prior is not None:
+            sent_back(prior)
         if back:
             gp, up = keep[m, :, :hidden], keep[m, :, hidden:]
             qv = grad_in[...]
@@ -233,38 +255,44 @@
                 res = dot_last(hid[...], mats[cols(k), :])
             else:
                 res = dot(hid[:, :hidden], down[:, cols(k)])
-            rsend[:, :, pl.ds(EXTRA + k * cw, cw)] = res.astype(BF16).reshape(peers, 8, cw)
+            rsend[:, :, rdata(k)] = res.astype(BF16).reshape(peers, 8, cws[k])
             fan_out(rsend, rrec, q, rcols(k, back), s_rsend, s_rrec.at[q * CHUNKS + k])
+
+    def collect(m, back):
+        q = m + (MICRO if back else 0)
+        both = tables(m)
         if back:
             xf = xa[m].astype(F32)
             sc = lax.rsqrt(jnp.sum(xf * xf, axis=1, keepdims=True) / width + EPS)
         coef = None
         kap_own = None
-        live = lax.broadcasted_iota(jnp.int32, (peers, 8, cw), 1) < 2 * CAP
+
+        def summed(sl, n):
+            got = rrec[q, :, :, sl]
+            live = lax.broadcasted_iota(jnp.int32, (peers, 8, n), 1) < 2 * CAP
+            got = jnp.where(live, got, jnp.zeros_like(got)).reshape(slots, n)
+            return dot(both, got)
+
         for k in range(CHUNKS + 1):
             if k < CHUNKS:
                 i = q * CHUNKS + k
                 wait_all(rrec.at[q, :, pl.ds(0, 2 * CAP), rcols(k, back)], s_rrec.at[i])
-                got = rrec[q, :, :, pl.ds(EXTRA + k * cw, cw)]
-                got = jnp.where(live, got, jnp.zeros_like(got)).reshape(slots, cw)
-                term = dot(both, got)
+                term = summed(rdata(k), cws[k])
                 part[:, cols(k)] = term[:ROWS]
-                szs[q, :, pl.ds(EXTRA + k * cw, cw)] = term[ROWS:].astype(BF16)
+                szs[q, :, rdata(k)] = term[ROWS:].astype(BF16)
                 if back and k == 0:
-                    kr = rrec[q, :, :, :EXTRA]
-                    kr = jnp.where(live[:, :, :EXTRA], kr, jnp.zeros_like(kr)).reshape(slots, EXTRA)
-                    kt = dot(both, kr)
+                    kt = summed(pl.ds(0, EXTRA), EXTRA)
                     kap_own = kt[:ROWS]
                     szs[q, :, :EXTRA] = kt[ROWS:].astype(BF16)
                 pltpu.make_async_remote_copy(
-                    szs.at[q, :, rcols(k, back)], szr.at[q, :, rcols(k, back)], s_szs,
+                    szs.at[q, :, rcols(k, back)], szr.at[q, :, rcols(k, back)], s_szs.at[q],
                     s_szr.at[i], device_id=partner, device_id_type=MESH,
                 ).start()
             if k > 0:
                 j = k - 1
                 i = q * CHUNKS + j
                 wait_all(szr.at[q, :, rcols(j, back)], s_szr.at[i])
-                add = part[:, cols(j)] + szr[q, :, pl.ds(EXTRA + j * cw, cw)].astype(F32)
+                add = part[:, cols(j)] + szr[q, :, rdata(j)].astype(F32)
                 base = xa[q, :, cols(j)].astype(F32)
                 if back:
                     if j == 0:
@@ -279,12 +307,12 @@
 
                 def pass_on(st):
                     pltpu.make_async_remote_copy(
-                        outs.at[q, :, cols(j)], xa.at[q, :, cols(j)], s_pga,
-                        s_in_a.at[i], device_id=same(st), device_id_type=MESH,
+                        outs.at[q, :, cols(j)], xb.at[q, :, cols(j)], s_pgb.at[q],
+                        s_in_b.at[i], device_id=other(st), device_id_type=MESH,
                     ).start()
                     pltpu.make_async_remote_copy(
-                        outs.at[q, :, cols(j)], xb.at[q, :, cols(j)], s_pgb,
-                        s_in_b.at[i], device_id=other(st), device_id_type=MESH,
+                        outs.at[q, :, cols(j)], xa.at[q, :, cols(j)], s_pga.at[q],
+                        s_in_a.at[i], device_id=same(st), device_id_type=MESH,
                     ).start()
 
                 if back:
@@ -298,33 +326,60 @@
                     def _():
                         pass_on(stage + 1)
 
-        target = seg_grad if back else seg_out
-        pltpu.make_async_copy(outs.at[q], target.at[0, mrow, :], s_out.at[q]).start()
-        wait_all(dsend.at[pl.ds(0, peers - 1), pl.ds(0, 2 * CAP), :], s_dsend)
-        if back:
-            wait_all(rsend.at[pl.ds(0, peers - 1), pl.ds(0, 2 * CAP), :], s_rsend)
-            wait_all(szs.at[q], s_szs)
-        else:
-            wait_all(rsend.at[pl.ds(0, peers - 1), pl.ds(0, 2 * CAP), pl.ds(EXTRA, width)], s_rsend)
-            wait_all(szs.at[q, :, pl.ds(EXTRA, width)], s_szs)
-        passes = (stage > 0) if back else (stage < stages - 1)
-
-        @pl.when(passes)
-        def _():
-            wait_all(outs.at[q], s_pga)
-            wait_all(outs.at[q], s_pgb)
-
-    @pl.loop(0, MICRO)
+            if k < CHUNKS:
+                yield
+        mrow = pl.ds(pl.multiple_of(m * ROWS, ROWS), ROWS)
+        pltpu.make_async_copy(outs.at[q], seg_both.at[int(back), mrow, :], s_out.at[q]).start()
+
+    def run(first, second=None, order=ORDER):
+        if second is not None:
+            for c in order:
+                next(first if c == "C" else second, None)
+        for g in (first, second):
+            if g is not None:
+                for _ in g:
+                    pass
+
+    run(dispatch(0, False, False))
+    for c in load:
+        c.wait()
+    eye_r = lax.broadcasted_iota(jnp.int32, (128, 128), 0)
+    eye_c = lax.broadcasted_iota(jnp.int32, (128, 128), 1)
+
+    @pl.loop(0, width // 128)
+    def _(i):
+        r = pl.ds(pl.multiple_of(i * 128, 128), 128)
+        col = jnp.sum(jnp.where(eye_r == eye_c, gain[:, r], 0.0), axis=1, keepdims=True)
+        mats[r, :] = (mats[r, :].astype(F32) * col).astype(BF16)
+
+    expert(0, False, None)
+
+    @pl.loop(0, MICRO - 1)
     def _(m):
-        section(m, False)
+        run(collect(m, False), dispatch(m + 1, False, True))
+        expert(m + 1, False, False)
 
     @pl.when(stage == stages - 1)
     def _():
         feed(cotangent, MICRO)
-
-    @pl.loop(0, MICRO)
+        run(dispatch(0, True, True))
+
+    run(collect(MICRO - 1, False))
+
+    @pl.when(stage < stages - 1)
+    def _():
+        run(dispatch(0, True, True))
+
+    expert(0, True, False)
+
+    @pl.loop(0, MICRO - 1)
     def _(m):
-        section(m, True)
+        run(collect(m, True), dispatch(m + 1, True, True))
+        expert(m + 1, True, True)
+
+    run(collect(MICRO - 1, True))
+    wait_all(dsend.at[pl.ds(0, peers - 1), pl.ds(0, 2 * CAP), :], s_dsend)
+    sent_back(True)
 
     grec[me] = gacc[...]
 
@@ -353,9 +408,19 @@
     def _():
         wait_all(cotangent, s_g.at[2])
 
-    @pl.loop(0, 2 * MICRO)
-    def _(q):
+    def left(q, sl, passes):
         wait_all(outs.at[q], s_out.at[q])
+        wait_all(szs.at[q, :, sl], s_szs.at[q])
+
+        @pl.when(passes)
+        def _():
+            wait_all(outs.at[q], s_pga.at[q])
+            wait_all(outs.at[q], s_pgb.at[q])
+
+    @pl.loop(0, MICRO)
+    def _(m):
+        left(m, pl.ds(EXTRA, width), stage < stages - 1)
+        left(m + MICRO, pl.ds(0, EXTRA + width), stage > 0)
 
 
 def body(tokens, cotangent, owner_ids, gate_weights, norm_gain, w_gate, w_up, w_down):
@@ -365,19 +430,19 @@
     slots = peers * 8
     rows = MICRO * ROWS
     wide = EXTRA + width
-    gain_col = norm_gain.reshape(width, 1)
+    ids = jnp.swapaxes(owner_ids, 1, 2)
+    gates = jnp.swapaxes(gate_weights, 1, 2)
     hbm = pl.BlockSpec(memory_space=pl.ANY)
     vmem = pl.BlockSpec(memory_space=pltpu.VMEM)
     dma = pltpu.SemaphoreType.DMA
-    seg_out, seg_grad, weighted = pl.pallas_call(
+    both, weighted = pl.pallas_call(
         kernel,
         out_shape=(
-            jax.ShapeDtypeStruct((1, rows, width), BF16),
-            jax.ShapeDtypeStruct((1, rows, width), BF16),
+            jax.ShapeDtypeStruct((2, rows, width), BF16),
             jax.ShapeDtypeStruct((1, width), F32),
         ),
         in_specs=[hbm, hbm, vmem, vmem, vmem, hbm, hbm, hbm],
-        out_specs=(hbm, hbm, vmem),
+        out_specs=(hbm, vmem),
         scratch_shapes=[
             pltpu.VMEM((width, 2 * hidden), BF16),
             pltpu.VMEM((hidden, width), BF16),
@@ -409,9 +474,9 @@
             dma((2 * MICRO * CHUNKS,)),
             dma,
             dma,
-            dma,
-            dma,
-            dma,
+            dma((2 * MICRO,)),
+            dma((2 * MICRO,)),
+            dma((2 * MICRO,)),
             dma((3,)),
             dma((2,)),
             dma((2 * MICRO,)),
@@ -421,8 +486,8 @@
             collective_id=0, has_side_effects=True, vmem_limit_bytes=56 << 20
         ),
         name="relay",
-    )(tokens, cotangent, owner_ids, gate_weights, gain_col, w_gate, w_up, w_down)
-    return (seg_out, seg_grad, weighted / norm_gain)
+    )(tokens, cotangent, ids, gates, norm_gain, w_gate, w_up, w_down)
+    return (both[0:1], both[1:2], weighted / norm_gain)
 
 
 def solution(mesh):

time: 501 us -> 420 us (0.84)
  Pallas kernels: 490 us -> 416 us
  local copies, waits for them, and re-layouts: 8.63 us -> 2.3 us
    pallas_call x1, Pallas kernels: 490 us -> 416 us  [body(): pl.pallas_call(kernel, out_shape=(jax.ShapeDtypeStruct((2, rows, width),...]
    unnamed x6 -> x4, local copies, waits for them, and re-layouts: 6.59 us -> 0.01 us
where the time goes in v2:
time: 420 us; the launch traced here: 419 us
  Pallas kernels  416 us (99%)
    pallas_call x1, Pallas kernels, body(): pl.pallas_call(kernel, out_shape=(jax.ShapeDtypeStruct((2, rows, width),...  416 us

profile of v2, /device:TPU:1, one launch (start us, length us, event | category | flops | bytes accessed | tf_op | source)
XLA Modules:
  0.0 419.4 jit_solution(1539904241645216405)
XLA Ops:
  0.6 415.8 %relay.1 = (bf16[2,128,2048]{2,1,0:T(8,128)(2,1)}, f32[1,2048]{1,0:T(1,128)}) custom-call(bf16[128,2048]{1,0:T(8,128)(2,1)} %tokens.1, bf16[128,2048]{1,0:T(8,128)(2,1)} %cotangent.1, s32[1,4,128]{2,1,0:T(4,128)} %bitcast.2, bf16[1,4,128]{2,1,0:T(4,128)(2,1)} %bitcast.3, f32[1,2048]{1,0:T(1,128)} %gain.1, bf16[1,1,2048,384]{3,2,1,0:T(8,128)(2,1)} %w_gate.1, ...), custom_call_target="tpu_custom_call" | custom-call | tf_op jit(solution)/shard_map/relay/pallas_call | solution.py:438
  416.4 0.0 copy-start
  416.5 0.0 copy-start.1
  416.5 2.3 fusion
  418.8 0.0 copy-done
  418.8 0.0 copy-done.1
  418.8 0.6 div.3
Async XLA Ops:
  416.4 2.3 copy-start
  416.5 2.3 copy-start.1
